TPU v7x, 32 devices: a whole 2x2x4 slice. The times are simulated.
32 devices in a mesh: groups: 2 (over y), tm: 16 (over z, x, core).
Axes of the slice: x: 2, y: 2, z: 4, core: 2. Of those that a mesh axis runs over, the one named last changes fastest.
Arguments:
- voltages: bfloat16 [256, 256, 2, 188], P(None, ('groups', 'tm')), parts along dimension 1, as said below
- off_starts: int32 [16], P('groups'), parts along dimension 0, may hold values from 0 to 124, as said below
- pointing: int32 [36], replicated, may hold values from 0 to 2047, as said below
- patterns: bfloat16 [2, 188, 2048], P(None, None, 'tm'), may hold values from -0.3125 to 0.3125
Outputs:
- beam_weights: bfloat16 [512, 2, 6768], P(('groups', 'tm')), parts along dimension 0
- beam_maps: float32 [512, 36, 2048], P('groups', None, 'tm'), parts along dimension 0
There are 2 independent parts, one for each index of `groups`. A program takes and returns all parts, laid end to end along the dimension named above; an argument that names none is the same for every part. Nothing has to cross between parts.
Inputs may be any that keep to these rules, and one draw needn't show every extreme that they name: Complex port voltages: thermal noise whose power differs between ports and grows along time, plus sky signals common to the ports. `off_starts`: each of the 8 off-source ranges covers 4 samples from this start; ranges may intersect. `pointing`: several beams may point at the same pixel.
All inputs are finite; a program needn't handle non-finite values.
Results may differ from a plain program's by a relative error of at most 0.0034.
Values may be sent and summed in bfloat16 or wider, within the bound.
No kernel may reach another device: no remote copies, remote signals or barrier semaphores. Data moves between devices by JAX's collectives and lax.ppermute only.
A program may use at most 64 MiB of HBM per device.

v0:
```python
import jax
import jax.numpy as jnp
from jax import lax
from jax.sharding import PartitionSpec as P

ITERS = 20
highest = lax.Precision.HIGHEST


def off_flags(moments, starts, range_len):
    shape_now = moments.shape
    flat_moments = moments.reshape(-1)
    inside = (flat_moments[None, :] >= starts[:, None]) & (
        flat_moments[None, :] < starts[:, None] + range_len
    )
    return jnp.any(inside, axis=0).reshape(shape_now)


def split_gram(products, port_count):
    corr_real = products[..., :port_count, :port_count] + products[..., port_count:, port_count:]
    corr_imag = products[..., port_count:, :port_count] - products[..., :port_count, port_count:]
    return jnp.stack([corr_real, corr_imag], axis=-3)


def beam_power(weights, patterns):
    port_count = weights.shape[3]
    real_rows = jnp.concatenate([weights[:, 0], weights[:, 1]], axis=-1)
    imag_rows = jnp.concatenate([-weights[:, 1], weights[:, 0]], axis=-1)
    rows_all = jnp.stack([real_rows, imag_rows], axis=2).reshape(-1, 2 * port_count)
    response = jnp.dot(
        rows_all, patterns.reshape(2 * port_count, -1), preferred_element_type=jnp.float32
    )
    response = response.reshape(weights.shape[0], weights.shape[2], 2, -1)
    return response[:, :, 0] * response[:, :, 0] + response[:, :, 1] * response[:, :, 1]


def on_device(voltages, off_starts, pointing, patterns):
    devices = lax.axis_size("tm")
    position = lax.axis_index("tm")
    channels = voltages.shape[0]
    samples_dev = voltages.shape[1]
    ports = voltages.shape[3]
    beams = pointing.shape[0]
    per_dev = channels // devices
    double_width = 2 * ports
    total_time = samples_dev * devices
    off_span = max(4, total_time // 32)
    every_moment = jnp.arange(total_time, dtype=jnp.int32)
    off_count = jnp.sum(off_flags(every_moment, off_starts, off_span).astype(jnp.float32))
    pixels = patterns.shape[2]
    pixel_ids = position * pixels + jnp.arange(pixels, dtype=jnp.int32)
    selector = (pixel_ids[:, None] == pointing[None, :]).astype(jnp.bfloat16)
    steer_local = jnp.einsum("rpx,xb->rpb", patterns, selector, preferred_element_type=jnp.float32)
    steering = lax.psum(steer_local, "tm")
    blocks = voltages.reshape(devices, per_dev, samples_dev, double_width)
    arrived = lax.all_to_all(blocks, "tm", split_axis=0, concat_axis=0, tiled=True)
    moments = (
        jnp.arange(devices, dtype=jnp.int32)[:, None] * samples_dev
        + jnp.arange(samples_dev, dtype=jnp.int32)[None, :]
    )
    is_off = off_flags(moments, off_starts, off_span)
    on_source = jnp.where(is_off[:, None, :, None], jnp.zeros_like(arrived), arrived)
    products = jnp.einsum("nksi,nksj->kij", on_source, arrived, preferred_element_type=jnp.float32)
    corr_mine = split_gram(products, ports)
    squared = jnp.square(arrived.astype(jnp.float32))
    powers = jnp.sum(jnp.where(is_off[:, None, :, None], squared, jnp.float32(0.0)), axis=(0, 2))
    noise_total = powers[:, :ports] + powers[:, ports:]
    noise_power = noise_total / off_count + 1e-06
    scales = 1.0 / jnp.sqrt(noise_power)
    white_real = corr_mine[:, 0] * scales[:, :, None] * scales[:, None, :]
    white_imag = corr_mine[:, 1] * scales[:, :, None] * scales[:, None, :]
    steer_real = steering[0][None]
    steer_imag = steering[1][None]

    def apply_white(matrix, vector):
        return jnp.einsum("kij,kjb->kib", matrix, vector, precision=highest)

    def power_turn(counter, state_pair):
        beam_real, beam_imag = state_pair
        conj_real = steer_real * beam_real + steer_imag * beam_imag
        conj_imag = steer_real * beam_imag - steer_imag * beam_real
        mixed_real = apply_white(white_real, conj_real) - apply_white(white_imag, conj_imag)
        mixed_imag = apply_white(white_real, conj_imag) + apply_white(white_imag, conj_real)
        image_real = steer_real * mixed_real - steer_imag * mixed_imag
        image_imag = steer_real * mixed_imag + steer_imag * mixed_real
        mean_square = (
            jnp.sum(image_real * image_real, axis=1) + jnp.sum(image_imag * image_imag, axis=1)
        ) / (2 * ports)
        factor = 1.0 / jnp.sqrt(mean_square + 1e-06)
        return (image_real * factor[:, None, :], image_imag * factor[:, None, :])

    initial = (
        jnp.broadcast_to(steer_real, (per_dev, ports, beams)),
        jnp.broadcast_to(steer_imag, (per_dev, ports, beams)),
    )
    beam_real, beam_imag = lax.fori_loop(0, ITERS, power_turn, initial)
    weight_real = beam_real * scales[:, :, None]
    weight_imag = beam_imag * scales[:, :, None]
    weight_pair = (
        jnp.stack([weight_real, weight_imag], axis=1).transpose(0, 1, 3, 2).astype(jnp.bfloat16)
    )
    flat_pair = weight_pair.reshape(per_dev, 2, beams * ports)
    collected = lax.all_gather(flat_pair, "tm", axis=0, tiled=True)
    all_weights = collected.reshape(channels, 2, beams, ports)
    maps_out = beam_power(all_weights, patterns)
    return (flat_pair, maps_out)


def solution(mesh):
    in_specs = (P(None, ("groups", "tm"), None, None), P("groups"), P(), P(None, None, "tm"))
    out_specs = (P(("groups", "tm"), None, None), P("groups", None, "tm"))
    return jax.shard_map(
        on_device, mesh=mesh, in_specs=in_specs, out_specs=out_specs, check_vma=False
    )
```

profile of v0, /device:TPU:0, one launch (start us, length us, event | category | flops | bytes accessed | tf_op | source)
XLA Modules:
  0.0 552.6 jit_solution(12295495400840213857)
XLA Ops:
  7.2 7.9 %copy.28 = bf16[256,8,2,188]{3,2,1,0:T(2,128)(2,1)S(1)} copy(bf16[256,8,2,188]{0,2,3,1:T(2,128)(2,1)} %param.6) | data formatting | bytes 3080192 | tf_op args[0]
  17.1 7.4 %all-to-all-start = ((bf16[16,16,8,376]{3,2,1,0:T(8,128)(2,1)}), bf16[16,16,8,376]{3,2,1,0:T(8,128)(2,1)S(1)}, u32[]{:S(2)}, u32[]{:S(2)}) async-start(bf16[16,16,8,376]{3,2,1,0:T(8,128)(2,1)} %reshape.61), calls=%async_computation | async-start | bytes 3145728 | tf_op jit(solution)/shard_map/all_to_all | solution.py:56
  25.1 81.9 %psum.7 = f32[2,188,36]{1,2,0:T(8,128)S(1)} all-reduce(f32[2,188,36]{1,2,0:T(8,128)S(1)} %convolution_bitcast_fusion.1), channel_id=1, replica_groups=mesh['groups'=2,'tm'=16] {'tm'}, use_global_device_ids=true, to_apply=%region_0.0 | all-reduce | flops 13536 | bytes 108288 | tf_op jit(solution)/shard_map/psum | solution.py:54
  110.7 3.6 fusion.11
  116.0 321.7 %while.12 = (s32[]{:T(128)}, f32[16,188,36]{1,2,0:T(8,128)}, f32[16,188,36]{1,2,0:T(8,128)}, f32[1,188,36]{1,2,0:T(8,128)S(1)}, f32[1,188,36]{1,2,0:T(8,128)S(1)...) while((s32[]{:T(128)}, f32[16,188,36]{1,2,0:T(8,128)}, f32[16,188,36]{1,2,0:T(8,128)}, ...), condition=%wide.region_8.9_spmd, body=%wide.region_5.8_spmd.sunk | while | flops 980656704 | bytes 30075944 | solution.py:96
  116.0 5.4 fusion.50
  127.6 3.2 multiply_reduce_fusion.3
  132.1 5.4 fusion.50
  143.7 3.2 multiply_reduce_fusion.3
  148.2 5.4 fusion.50
  159.8 3.2 multiply_reduce_fusion.3
  164.3 5.4 fusion.50
  175.8 3.2 multiply_reduce_fusion.3
  180.4 5.4 fusion.50
  191.9 3.2 multiply_reduce_fusion.3
  196.4 5.4 fusion.50
  208.0 3.2 multiply_reduce_fusion.3
  212.5 5.4 fusion.50
  224.1 3.2 multiply_reduce_fusion.3
  228.6 5.4 fusion.50
  240.2 3.2 multiply_reduce_fusion.3
  244.7 5.4 fusion.50
  256.3 3.2 multiply_reduce_fusion.3
  260.8 5.4 fusion.50
  272.3 3.2 multiply_reduce_fusion.3
  276.9 5.4 fusion.50
  292.9 5.4 fusion.50
  304.5 3.2 multiply_reduce_fusion.3
  309.0 5.4 fusion.50
  325.1 5.4 fusion.50
  336.7 3.2 multiply_reduce_fusion.3
  341.2 5.4 fusion.50
  357.3 5.4 fusion.50
  368.9 3.2 multiply_reduce_fusion.3
  373.4 5.4 fusion.50
  384.9 3.2 multiply_reduce_fusion.3
  389.5 5.4 fusion.50
  401.0 3.2 multiply_reduce_fusion.3
  405.5 5.4 fusion.50
  417.1 3.2 multiply_reduce_fusion.3
  421.6 5.4 fusion.50
  433.2 3.2 multiply_reduce_fusion.3
  442.7 60.5 %all-gather.2.cloned.1.call-done = bf16[256,2,6768]{2,0,1:T(8,128)(2,1)} async-done(((bf16[16,2,6768]{2,0,1:T(8,128)(2,1)}), bf16[256,2,6768]{2,0,1:T(8,128)(2,1)}) %all-gather.2.cloned.1.call-update) | async-done | bytes 6930448 | tf_op jit(solution)/shard_map/all_gather | solution.py:103
  503.3 10.1 %copy.29 = bf16[256,2,6768]{0,2,1:T(8,128)(2,1)} copy(bf16[256,2,6768]{2,0,1:T(8,128)(2,1)} %all-gather.2.cloned.1.call-done) | data formatting | bytes 13860864 | tf_op jit(solution)/shard_map/all_gather | solution.py:103
  513.4 9.9 %reshape.63 = bf16[256,2,36,188]{0,3,2,1:T(8,128)(2,1)} reshape(bf16[256,2,6768]{0,2,1:T(8,128)(2,1)} %copy.29) | data formatting | bytes 13860864 | tf_op jit(solution)/shard_map/reshape | solution.py:104
  523.3 3.7 slice_bitcast_fusion
  528.6 7.0 %maximum_bitcast_fusion = (bf16[256,36,1,376]{0,3,2,1:T(8,128)(2,1)}, bf16[256,36,1,376]{0,3,2,1:T(8,128)(2,1)}) fusion(bf16[256,36,188]{0,2,1:T(8,128)(2,1)S(1)} %get-tuple-element.71, bf16[256,36,188]{0,2,1:T(8,128)(2,1)S(1)} %get-tuple-element.72, bf16[256,36,188]{0,2,1:T(8,128)(2,1)S(1)} %fusion.32), kind=kLoop, calls=%fused_computation.19 | loop fusion | flops 27721728 | bytes 24256512 | tf_op jit(solution)/shard_map/stack | solution.py:29
  535.6 7.2 %fusion.4 = f32[256,36,2,128]{3,0,2,1:T(8,128)S(1)} fusion(bf16[256,36,1,376]{0,3,2,1:T(8,128)(2,1)} %get-tuple-element.74, bf16[256,36,1,376]{0,3,2,1:T(8,128)(2,1)} %get-tuple-element.73, bf16[376,128,1,1]{1,0,2,3:T(8,128)(2,1)S(1)} %reshape.67), kind=kOutput, calls=%fused_computation.15 | convolution fusion | flops 1781121024 | bytes 23394304 | tf_op jit(solution)/shard_map/dot_general | solution.py:30
  (238 shorter events, 175.2 us)
Async XLA Ops:
  15.1 9.6 %copy-start.6 = (s32[8]{0:T(128)S(1)}, s32[8]{0:T(128)}, u32[]{:S(2)}) copy-start(s32[8]{0:T(128)} %param.7) | copy-start | bytes 100
  15.1 9.8 %copy-start.4 = (bf16[2,188,128]{2,0,1:T(2,128)(2,1)S(1)}, bf16[2,188,128]{2,0,1:T(2,128)(2,1)}, u32[]{:S(2)}) copy-start(bf16[2,188,128]{2,0,1:T(2,128)(2,1)} %param.9) | copy-start | bytes 288772
  15.1 9.8 %copy-start.5 = (s32[36]{0:T(128)S(1)}, s32[36]{0:T(128)}, u32[]{:S(2)}) copy-start(s32[36]{0:T(128)} %param.8) | copy-start | bytes 436
  17.1 90.5 %all-to-all-start = ((bf16[16,16,8,376]{3,2,1,0:T(8,128)(2,1)}), bf16[16,16,8,376]{3,2,1,0:T(8,128)(2,1)S(1)}, u32[]{:S(2)}, u32[]{:S(2)}) async-start(bf16[16,16,8,376]{3,2,1,0:T(8,128)(2,1)} %reshape.61), calls=%async_computation | async-start | bytes 3145728 | tf_op jit(solution)/shard_map/all_to_all | solution.py:56
  24.5 478.8 %all-gather.2.cloned.1.call-start = ((), (), s32[]{:S(2)}) async-start(), calls=%async_computation.1 | async-start | bytes 7380992 | tf_op jit(solution)/shard_map/all_gather | solution.py:103
  116.0 5.4 copy-start.1
  116.0 5.4 copy-start.2
  132.1 5.4 copy-start.1
  132.1 5.4 copy-start.2
  148.2 5.4 copy-start.1
  148.2 5.4 copy-start.2
  153.6 3.1 copy-start
  164.3 5.4 copy-start.1
  164.3 5.4 copy-start.2
  180.4 5.4 copy-start.1
  180.4 5.4 copy-start.2
  185.8 3.1 copy-start
  196.4 5.4 copy-start.1
  196.4 5.4 copy-start.2
  212.5 5.4 copy-start.1
  212.5 5.4 copy-start.2
  228.6 5.4 copy-start.1
  228.6 5.4 copy-start.2
  244.7 5.4 copy-start.1
  244.7 5.4 copy-start.2
  260.8 5.4 copy-start.1
  260.8 5.4 copy-start.2
  276.9 5.4 copy-start.1
  276.9 5.4 copy-start.2
  292.9 5.4 copy-start.1
  292.9 5.4 copy-start.2
  309.0 5.4 copy-start.1
  309.0 5.4 copy-start.2
  325.1 5.4 copy-start.1
  325.1 5.4 copy-start.2
  341.2 5.4 copy-start.1
  341.2 5.4 copy-start.2
  357.3 5.4 copy-start.1
  357.3 5.4 copy-start.2
  373.4 5.4 copy-start.1
  373.4 5.4 copy-start.2
  389.4 5.4 copy-start.1
  389.5 5.4 copy-start.2
  405.5 5.4 copy-start.1
  405.5 5.4 copy-start.2
  421.6 5.4 copy-start.1
  421.6 5.4 copy-start.2
  523.3 5.1 copy-start.3
  (18 other events, 55.7 us)
Sparse Core Ops, SparseCore 0:
  440.7 62.5 all-gather.1
where the time goes:
time: 553 us
  matrix products  303 us (55%)
  blocking collectives  81.9 us (15%)
  waiting for transfers between devices  60.6 us (11%)
  other arithmetic  43.2 us (8%)
  local copies, waits for them, and re-layouts  40.7 us (7%)
  between operations  14.2 us (3%)
  starting transfers between devices  7.43 us (1%)
    dot_general x80, matrix products, apply_white(): return jnp.einsum('kij,kjb->kib', matrix, vector, precision=highest)  294 us
    psum x1, blocking collectives, on_device(): steering = lax.psum(steer_local, 'tm')  81.9 us
    all_gather x1, waiting for transfers between devices, on_device(): collected = lax.all_gather(flat_pair, 'tm', axis=0, tiled=True)  60.5 us
    mul x20, other arithmetic, power_turn(): return (image_real * factor[:, None, :], image_imag * factor[:, None, :])  25.8 us
    unnamed x11, local copies, waits for them, and re-layouts  11.5 us
  transfers between devices with their start and end apart: 2, of which 1 were waited for; matrix products, arithmetic and copies ran while one was open for 1% of the time, Pallas kernels for 0%

commit v1 on v0

--- a/solution.py
+++ b/solution.py
@@ -51,7 +51,9 @@
     pixel_ids = position * pixels + jnp.arange(pixels, dtype=jnp.int32)
     selector = (pixel_ids[:, None] == pointing[None, :]).astype(jnp.bfloat16)
     steer_local = jnp.einsum("rpx,xb->rpb", patterns, selector, preferred_element_type=jnp.float32)
-    steering = lax.psum(steer_local, "tm")
+    steering = steer_local
+    for hop in (1, 2, 4, 8):
+        steering = steering + lax.ppermute(steering, "tm", [(dev, dev ^ hop) for dev in range(16)])
     blocks = voltages.reshape(devices, per_dev, samples_dev, double_width)
     arrived = lax.all_to_all(blocks, "tm", split_axis=0, concat_axis=0, tiled=True)
     moments = (

time: 553 us -> 514 us (0.929)
  blocking collectives: 81.9 us -> 0 us
  waiting for transfers between devices: 60.6 us -> 95.5 us
  starting transfers between devices: 7.43 us -> 14.3 us
    psum x1 -> x0, blocking collectives: 81.9 us -> none  [on_device(): steering = lax.psum(steer_local, 'tm')]
    ppermute x0 -> x4, waiting for transfers between devices: none -> 33.2 us  [on_device(): lax.ppermute(steering, 'tm', [(dev, dev ^ hop) for dev in range(16)])]
    ppermute x0 -> x4, starting transfers between devices: none -> 6.85 us  [on_device(): lax.ppermute(steering, 'tm', [(dev, dev ^ hop) for dev in range(16)])]
  transfers between devices with their start and end apart: 2 -> 6, of which waited for: 1 -> 5; matrix products, arithmetic and copies ran while one was open for 1% -> 1% of each run, Pallas kernels for 0% -> 0%
where the time goes in v1:
time: 514 us; the launch traced here: 513 us
  matrix products  303 us (59%)
  waiting for transfers between devices  95.5 us (19%)
  other arithmetic  43.7 us (9%)
  local copies, waits for them, and re-layouts  40.6 us (8%)
  starting transfers between devices  14.3 us (3%)
  between operations  14.2 us (3%)
    dot_general x80, matrix products, apply_white(): return jnp.einsum('kij,kjb->kib', matrix, vector, precision=highest)  294 us
    all_gather x1, waiting for transfers between devices, on_device(): collected = lax.all_gather(flat_pair, 'tm', axis=0, tiled=True)  62.3 us
    ppermute x4, waiting for transfers between devices, on_device(): lax.ppermute(steering, 'tm', [(dev, dev ^ hop) for dev in range(16)])  33.2 us
    mul x20, other arithmetic, power_turn(): return (image_real * factor[:, None, :], image_imag * factor[:, None, :])  26.1 us
    unnamed x11, local copies, waits for them, and re-layouts  11.5 us
  transfers between devices with their start and end apart: 6, of which 5 were waited for; matrix products, arithmetic and copies ran while one was open for 1% of the time, Pallas kernels for 0%

profile of v1, /device:TPU:0, one launch (start us, length us, event | category | flops | bytes accessed | tf_op | source)
XLA Modules:
  0.0 513.0 jit_solution(11280824664189523284)
XLA Ops:
  7.2 7.9 %copy.28 = bf16[256,8,2,188]{3,2,1,0:T(2,128)(2,1)S(1)} copy(bf16[256,8,2,188]{0,2,3,1:T(2,128)(2,1)} %param.6) | data formatting | bytes 3080192 | tf_op args[0]
  17.1 7.4 %all-to-all-start = ((bf16[16,16,8,376]{3,2,1,0:T(8,128)(2,1)}), bf16[16,16,8,376]{3,2,1,0:T(8,128)(2,1)S(1)}, u32[]{:S(2)}, u32[]{:S(2)}) async-start(bf16[16,16,8,376]{3,2,1,0:T(8,128)(2,1)} %reshape.61), calls=%async_computation | async-start | bytes 3145728 | tf_op jit(solution)/shard_map/all_to_all | solution.py:58
  28.1 10.7 %collective-permute-done.1 = f32[2,188,36]{1,2,0:T(8,128)S(1)} collective-permute-done((f32[2,188,36]{1,2,0:T(8,128)S(1)}, f32[2,188,36]{1,2,0:T(8,128)S(1)}, u32[]{:S(2)}, u32[]{:S(2)}) %collective-permute-start.1) | collective-permute-done | bytes 54176 | tf_op jit(solution)/shard_map/ppermute | solution.py:56
  39.0 13.8 %collective-permute-done.2 = f32[2,188,36]{1,2,0:T(8,128)S(1)} collective-permute-done((f32[2,188,36]{1,2,0:T(8,128)S(1)}, f32[2,188,36]{1,2,0:T(8,128)S(1)}, u32[]{:S(2)}, u32[]{:S(2)}) %collective-permute-start.2) | collective-permute-done | bytes 54176 | tf_op jit(solution)/shard_map/ppermute | solution.py:56
  52.8 4.4 collective-permute-start.3
  57.9 7.9 %collective-permute-done.3 = f32[2,188,36]{1,2,0:T(8,128)S(1)} collective-permute-done((f32[2,188,36]{1,2,0:T(8,128)S(1)}, f32[2,188,36]{1,2,0:T(8,128)S(1)}, u32[]{:S(2)}, u32[]{:S(2)}) %collective-permute-start.3) | collective-permute-done | bytes 54176 | tf_op jit(solution)/shard_map/ppermute | solution.py:56
  68.9 3.8 fusion.11
  74.4 321.9 %while.12 = (s32[]{:T(128)}, f32[16,188,36]{1,2,0:T(8,128)}, f32[16,188,36]{1,2,0:T(8,128)}, f32[1,188,36]{1,2,0:T(8,128)S(1)}, f32[1,188,36]{1,2,0:T(8,128)S(1)...) while((s32[]{:T(128)}, f32[16,188,36]{1,2,0:T(8,128)}, f32[16,188,36]{1,2,0:T(8,128)}, ...), condition=%wide.region_7.8_spmd, body=%wide.region_4.7_spmd.sunk | while | flops 980656704 | bytes 30075944 | solution.py:98
  74.4 5.4 %fusion.50 = f32[16,36,188]{2,1,0:T(8,128)S(1)} fusion(f32[16,188,188]{2,1,0:T(8,128)} %get-tuple-element.155, f32[16,188,36]{1,2,0:T(8,128)} %get-tuple-element.143, f32[16,188,36]{1,2,0:T(8,128)} %get-tuple-element.144, f32[188,36]{0,1:T(8,128)S(1)} %bitcast.63, f32[188,36]{0,1:T(8,128)S(1)} %bitcast.68), kind=kOutput, calls=%fused_computation.13.clone.1 | convolution fusion | flops 244622592 | bytes 3615616 | tf_op jit(solution)/shard_map/while/body/eval_jaxpr/kij,kjb->kib/dot_general | solution.py:78
  85.9 3.2 multiply_reduce_fusion.3
  90.5 5.4 %fusion.50 = f32[16,36,188]{2,1,0:T(8,128)S(1)} fusion(f32[16,188,188]{2,1,0:T(8,128)} %get-tuple-element.155, f32[16,188,36]{1,2,0:T(8,128)} %get-tuple-element.143, f32[16,188,36]{1,2,0:T(8,128)} %get-tuple-element.144, f32[188,36]{0,1:T(8,128)S(1)} %bitcast.63, f32[188,36]{0,1:T(8,128)S(1)} %bitcast.68), kind=kOutput, calls=%fused_computation.13.clone.1 | convolution fusion | flops 244622592 | bytes 3615616 | tf_op jit(solution)/shard_map/while/body/eval_jaxpr/kij,kjb->kib/dot_general | solution.py:78
  102.0 3.2 multiply_reduce_fusion.3
  106.6 5.4 %fusion.50 = f32[16,36,188]{2,1,0:T(8,128)S(1)} fusion(f32[16,188,188]{2,1,0:T(8,128)} %get-tuple-element.155, f32[16,188,36]{1,2,0:T(8,128)} %get-tuple-element.143, f32[16,188,36]{1,2,0:T(8,128)} %get-tuple-element.144, f32[188,36]{0,1:T(8,128)S(1)} %bitcast.63, f32[188,36]{0,1:T(8,128)S(1)} %bitcast.68), kind=kOutput, calls=%fused_computation.13.clone.1 | convolution fusion | flops 244622592 | bytes 3615616 | tf_op jit(solution)/shard_map/while/body/eval_jaxpr/kij,kjb->kib/dot_general | solution.py:78
  118.1 3.2 multiply_reduce_fusion.3
  122.7 5.4 %fusion.50 = f32[16,36,188]{2,1,0:T(8,128)S(1)} fusion(f32[16,188,188]{2,1,0:T(8,128)} %get-tuple-element.155, f32[16,188,36]{1,2,0:T(8,128)} %get-tuple-element.143, f32[16,188,36]{1,2,0:T(8,128)} %get-tuple-element.144, f32[188,36]{0,1:T(8,128)S(1)} %bitcast.63, f32[188,36]{0,1:T(8,128)S(1)} %bitcast.68), kind=kOutput, calls=%fused_computation.13.clone.1 | convolution fusion | flops 244622592 | bytes 3615616 | tf_op jit(solution)/shard_map/while/body/eval_jaxpr/kij,kjb->kib/dot_general | solution.py:78
  134.2 3.2 multiply_reduce_fusion.3
  138.8 5.4 %fusion.50 = f32[16,36,188]{2,1,0:T(8,128)S(1)} fusion(f32[16,188,188]{2,1,0:T(8,128)} %get-tuple-element.155, f32[16,188,36]{1,2,0:T(8,128)} %get-tuple-element.143, f32[16,188,36]{1,2,0:T(8,128)} %get-tuple-element.144, f32[188,36]{0,1:T(8,128)S(1)} %bitcast.63, f32[188,36]{0,1:T(8,128)S(1)} %bitcast.68), kind=kOutput, calls=%fused_computation.13.clone.1 | convolution fusion | flops 244622592 | bytes 3615616 | tf_op jit(solution)/shard_map/while/body/eval_jaxpr/kij,kjb->kib/dot_general | solution.py:78
  154.9 5.4 %fusion.50 = f32[16,36,188]{2,1,0:T(8,128)S(1)} fusion(f32[16,188,188]{2,1,0:T(8,128)} %get-tuple-element.155, f32[16,188,36]{1,2,0:T(8,128)} %get-tuple-element.143, f32[16,188,36]{1,2,0:T(8,128)} %get-tuple-element.144, f32[188,36]{0,1:T(8,128)S(1)} %bitcast.63, f32[188,36]{0,1:T(8,128)S(1)} %bitcast.68), kind=kOutput, calls=%fused_computation.13.clone.1 | convolution fusion | flops 244622592 | bytes 3615616 | tf_op jit(solution)/shard_map/while/body/eval_jaxpr/kij,kjb->kib/dot_general | solution.py:78
  166.4 3.2 multiply_reduce_fusion.3
  171.0 5.4 %fusion.50 = f32[16,36,188]{2,1,0:T(8,128)S(1)} fusion(f32[16,188,188]{2,1,0:T(8,128)} %get-tuple-element.155, f32[16,188,36]{1,2,0:T(8,128)} %get-tuple-element.143, f32[16,188,36]{1,2,0:T(8,128)} %get-tuple-element.144, f32[188,36]{0,1:T(8,128)S(1)} %bitcast.63, f32[188,36]{0,1:T(8,128)S(1)} %bitcast.68), kind=kOutput, calls=%fused_computation.13.clone.1 | convolution fusion | flops 244622592 | bytes 3615616 | tf_op jit(solution)/shard_map/while/body/eval_jaxpr/kij,kjb->kib/dot_general | solution.py:78
  187.1 5.4 %fusion.50 = f32[16,36,188]{2,1,0:T(8,128)S(1)} fusion(f32[16,188,188]{2,1,0:T(8,128)} %get-tuple-element.155, f32[16,188,36]{1,2,0:T(8,128)} %get-tuple-element.143, f32[16,188,36]{1,2,0:T(8,128)} %get-tuple-element.144, f32[188,36]{0,1:T(8,128)S(1)} %bitcast.63, f32[188,36]{0,1:T(8,128)S(1)} %bitcast.68), kind=kOutput, calls=%fused_computation.13.clone.1 | convolution fusion | flops 244622592 | bytes 3615616 | tf_op jit(solution)/shard_map/while/body/eval_jaxpr/kij,kjb->kib/dot_general | solution.py:78
  198.6 3.2 multiply_reduce_fusion.3
  203.2 5.4 %fusion.50 = f32[16,36,188]{2,1,0:T(8,128)S(1)} fusion(f32[16,188,188]{2,1,0:T(8,128)} %get-tuple-element.155, f32[16,188,36]{1,2,0:T(8,128)} %get-tuple-element.143, f32[16,188,36]{1,2,0:T(8,128)} %get-tuple-element.144, f32[188,36]{0,1:T(8,128)S(1)} %bitcast.63, f32[188,36]{0,1:T(8,128)S(1)} %bitcast.68), kind=kOutput, calls=%fused_computation.13.clone.1 | convolution fusion | flops 244622592 | bytes 3615616 | tf_op jit(solution)/shard_map/while/body/eval_jaxpr/kij,kjb->kib/dot_general | solution.py:78
  214.7 3.2 multiply_reduce_fusion.3
  219.3 5.4 %fusion.50 = f32[16,36,188]{2,1,0:T(8,128)S(1)} fusion(f32[16,188,188]{2,1,0:T(8,128)} %get-tuple-element.155, f32[16,188,36]{1,2,0:T(8,128)} %get-tuple-element.143, f32[16,188,36]{1,2,0:T(8,128)} %get-tuple-element.144, f32[188,36]{0,1:T(8,128)S(1)} %bitcast.63, f32[188,36]{0,1:T(8,128)S(1)} %bitcast.68), kind=kOutput, calls=%fused_computation.13.clone.1 | convolution fusion | flops 244622592 | bytes 3615616 | tf_op jit(solution)/shard_map/while/body/eval_jaxpr/kij,kjb->kib/dot_general | solution.py:78
  230.8 3.2 multiply_reduce_fusion.3
  235.3 5.4 %fusion.50 = f32[16,36,188]{2,1,0:T(8,128)S(1)} fusion(f32[16,188,188]{2,1,0:T(8,128)} %get-tuple-element.155, f32[16,188,36]{1,2,0:T(8,128)} %get-tuple-element.143, f32[16,188,36]{1,2,0:T(8,128)} %get-tuple-element.144, f32[188,36]{0,1:T(8,128)S(1)} %bitcast.63, f32[188,36]{0,1:T(8,128)S(1)} %bitcast.68), kind=kOutput, calls=%fused_computation.13.clone.1 | convolution fusion | flops 244622592 | bytes 3615616 | tf_op jit(solution)/shard_map/while/body/eval_jaxpr/kij,kjb->kib/dot_general | solution.py:78
  246.9 3.2 multiply_reduce_fusion.3
  251.4 5.4 %fusion.50 = f32[16,36,188]{2,1,0:T(8,128)S(1)} fusion(f32[16,188,188]{2,1,0:T(8,128)} %get-tuple-element.155, f32[16,188,36]{1,2,0:T(8,128)} %get-tuple-element.143, f32[16,188,36]{1,2,0:T(8,128)} %get-tuple-element.144, f32[188,36]{0,1:T(8,128)S(1)} %bitcast.63, f32[188,36]{0,1:T(8,128)S(1)} %bitcast.68), kind=kOutput, calls=%fused_computation.13.clone.1 | convolution fusion | flops 244622592 | bytes 3615616 | tf_op jit(solution)/shard_map/while/body/eval_jaxpr/kij,kjb->kib/dot_general | solution.py:78
  263.0 3.2 multiply_reduce_fusion.3
  267.5 5.4 %fusion.50 = f32[16,36,188]{2,1,0:T(8,128)S(1)} fusion(f32[16,188,188]{2,1,0:T(8,128)} %get-tuple-element.155, f32[16,188,36]{1,2,0:T(8,128)} %get-tuple-element.143, f32[16,188,36]{1,2,0:T(8,128)} %get-tuple-element.144, f32[188,36]{0,1:T(8,128)S(1)} %bitcast.63, f32[188,36]{0,1:T(8,128)S(1)} %bitcast.68), kind=kOutput, calls=%fused_computation.13.clone.1 | convolution fusion | flops 244622592 | bytes 3615616 | tf_op jit(solution)/shard_map/while/body/eval_jaxpr/kij,kjb->kib/dot_general | solution.py:78
  283.6 5.4 %fusion.50 = f32[16,36,188]{2,1,0:T(8,128)S(1)} fusion(f32[16,188,188]{2,1,0:T(8,128)} %get-tuple-element.155, f32[16,188,36]{1,2,0:T(8,128)} %get-tuple-element.143, f32[16,188,36]{1,2,0:T(8,128)} %get-tuple-element.144, f32[188,36]{0,1:T(8,128)S(1)} %bitcast.63, f32[188,36]{0,1:T(8,128)S(1)} %bitcast.68), kind=kOutput, calls=%fused_computation.13.clone.1 | convolution fusion | flops 244622592 | bytes 3615616 | tf_op jit(solution)/shard_map/while/body/eval_jaxpr/kij,kjb->kib/dot_general | solution.py:78
  295.2 3.2 multiply_reduce_fusion.3
  299.7 5.4 %fusion.50 = f32[16,36,188]{2,1,0:T(8,128)S(1)} fusion(f32[16,188,188]{2,1,0:T(8,128)} %get-tuple-element.155, f32[16,188,36]{1,2,0:T(8,128)} %get-tuple-element.143, f32[16,188,36]{1,2,0:T(8,128)} %get-tuple-element.144, f32[188,36]{0,1:T(8,128)S(1)} %bitcast.63, f32[188,36]{0,1:T(8,128)S(1)} %bitcast.68), kind=kOutput, calls=%fused_computation.13.clone.1 | convolution fusion | flops 244622592 | bytes 3615616 | tf_op jit(solution)/shard_map/while/body/eval_jaxpr/kij,kjb->kib/dot_general | solution.py:78
  315.8 5.4 %fusion.50 = f32[16,36,188]{2,1,0:T(8,128)S(1)} fusion(f32[16,188,188]{2,1,0:T(8,128)} %get-tuple-element.155, f32[16,188,36]{1,2,0:T(8,128)} %get-tuple-element.143, f32[16,188,36]{1,2,0:T(8,128)} %get-tuple-element.144, f32[188,36]{0,1:T(8,128)S(1)} %bitcast.63, f32[188,36]{0,1:T(8,128)S(1)} %bitcast.68), kind=kOutput, calls=%fused_computation.13.clone.1 | convolution fusion | flops 244622592 | bytes 3615616 | tf_op jit(solution)/shard_map/while/body/eval_jaxpr/kij,kjb->kib/dot_general | solution.py:78
  327.4 3.2 multiply_reduce_fusion.3
  331.9 5.4 %fusion.50 = f32[16,36,188]{2,1,0:T(8,128)S(1)} fusion(f32[16,188,188]{2,1,0:T(8,128)} %get-tuple-element.155, f32[16,188,36]{1,2,0:T(8,128)} %get-tuple-element.143, f32[16,188,36]{1,2,0:T(8,128)} %get-tuple-element.144, f32[188,36]{0,1:T(8,128)S(1)} %bitcast.63, f32[188,36]{0,1:T(8,128)S(1)} %bitcast.68), kind=kOutput, calls=%fused_computation.13.clone.1 | convolution fusion | flops 244622592 | bytes 3615616 | tf_op jit(solution)/shard_map/while/body/eval_jaxpr/kij,kjb->kib/dot_general | solution.py:78
  348.0 5.4 %fusion.50 = f32[16,36,188]{2,1,0:T(8,128)S(1)} fusion(f32[16,188,188]{2,1,0:T(8,128)} %get-tuple-element.155, f32[16,188,36]{1,2,0:T(8,128)} %get-tuple-element.143, f32[16,188,36]{1,2,0:T(8,128)} %get-tuple-element.144, f32[188,36]{0,1:T(8,128)S(1)} %bitcast.63, f32[188,36]{0,1:T(8,128)S(1)} %bitcast.68), kind=kOutput, calls=%fused_computation.13.clone.1 | convolution fusion | flops 244622592 | bytes 3615616 | tf_op jit(solution)/shard_map/while/body/eval_jaxpr/kij,kjb->kib/dot_general | solution.py:78
  359.6 3.2 multiply_reduce_fusion.3
  364.1 5.4 %fusion.50 = f32[16,36,188]{2,1,0:T(8,128)S(1)} fusion(f32[16,188,188]{2,1,0:T(8,128)} %get-tuple-element.155, f32[16,188,36]{1,2,0:T(8,128)} %get-tuple-element.143, f32[16,188,36]{1,2,0:T(8,128)} %get-tuple-element.144, f32[188,36]{0,1:T(8,128)S(1)} %bitcast.63, f32[188,36]{0,1:T(8,128)S(1)} %bitcast.68), kind=kOutput, calls=%fused_computation.13.clone.1 | convolution fusion | flops 244622592 | bytes 3615616 | tf_op jit(solution)/shard_map/while/body/eval_jaxpr/kij,kjb->kib/dot_general | solution.py:78
  380.2 5.4 %fusion.50 = f32[16,36,188]{2,1,0:T(8,128)S(1)} fusion(f32[16,188,188]{2,1,0:T(8,128)} %get-tuple-element.155, f32[16,188,36]{1,2,0:T(8,128)} %get-tuple-element.143, f32[16,188,36]{1,2,0:T(8,128)} %get-tuple-element.144, f32[188,36]{0,1:T(8,128)S(1)} %bitcast.63, f32[188,36]{0,1:T(8,128)S(1)} %bitcast.68), kind=kOutput, calls=%fused_computation.13.clone.1 | convolution fusion | flops 244622592 | bytes 3615616 | tf_op jit(solution)/shard_map/while/body/eval_jaxpr/kij,kjb->kib/dot_general | solution.py:78
  391.8 3.2 multiply_reduce_fusion.3
  401.3 62.3 %all-gather.2.cloned.1.call-done = bf16[256,2,6768]{2,0,1:T(8,128)(2,1)} async-done(((bf16[16,2,6768]{2,0,1:T(8,128)(2,1)}), bf16[256,2,6768]{2,0,1:T(8,128)(2,1)}) %all-gather.2.cloned.1.call-update) | async-done | bytes 6930448 | tf_op jit(solution)/shard_map/all_gather | solution.py:105
  463.6 10.1 %copy.29 = bf16[256,2,6768]{0,2,1:T(8,128)(2,1)} copy(bf16[256,2,6768]{2,0,1:T(8,128)(2,1)} %all-gather.2.cloned.1.call-done) | data formatting | bytes 13860864 | tf_op jit(solution)/shard_map/all_gather | solution.py:105
  473.7 9.9 %reshape.63 = bf16[256,2,36,188]{0,3,2,1:T(8,128)(2,1)} reshape(bf16[256,2,6768]{0,2,1:T(8,128)(2,1)} %copy.29) | data formatting | bytes 13860864 | tf_op jit(solution)/shard_map/reshape | solution.py:106
  483.6 3.7 slice_bitcast_fusion
  488.9 7.0 %maximum_bitcast_fusion = (bf16[256,36,1,376]{0,3,2,1:T(8,128)(2,1)}, bf16[256,36,1,376]{0,3,2,1:T(8,128)(2,1)}) fusion(bf16[256,36,188]{0,2,1:T(8,128)(2,1)S(1)} %get-tuple-element.71, bf16[256,36,188]{0,2,1:T(8,128)(2,1)S(1)} %get-tuple-element.72, bf16[256,36,188]{0,2,1:T(8,128)(2,1)S(1)} %fusion.32), kind=kLoop, calls=%fused_computation.19 | loop fusion | flops 27721728 | bytes 24256512 | tf_op jit(solution)/shard_map/stack | solution.py:29
  496.0 7.2 %fusion.4 = f32[256,36,2,128]{3,0,2,1:T(8,128)S(1)} fusion(bf16[256,36,1,376]{0,3,2,1:T(8,128)(2,1)} %get-tuple-element.74, bf16[256,36,1,376]{0,3,2,1:T(8,128)(2,1)} %get-tuple-element.73, bf16[376,128,1,1]{1,0,2,3:T(8,128)(2,1)S(1)} %reshape.67), kind=kOutput, calls=%fused_computation.15 | convolution fusion | flops 1781121024 | bytes 23394304 | tf_op jit(solution)/shard_map/dot_general | solution.py:30
  (249 shorter events, 188.4 us)
Async XLA Ops:
  15.1 9.5 %copy-start.4 = (bf16[2,188,128]{2,0,1:T(2,128)(2,1)S(1)}, bf16[2,188,128]{2,0,1:T(2,128)(2,1)}, u32[]{:S(2)}) copy-start(bf16[2,188,128]{2,0,1:T(2,128)(2,1)} %param.9) | copy-start | bytes 288772
  15.1 9.5 %copy-start.5 = (s32[36]{0:T(128)S(1)}, s32[36]{0:T(128)}, u32[]{:S(2)}) copy-start(s32[36]{0:T(128)} %param.8) | copy-start | bytes 436
  15.1 12.9 %copy-start.6 = (s32[8]{0:T(128)S(1)}, s32[8]{0:T(128)}, u32[]{:S(2)}) copy-start(s32[8]{0:T(128)} %param.7) | copy-start | bytes 100
  17.1 48.7 %all-to-all-start = ((bf16[16,16,8,376]{3,2,1,0:T(8,128)(2,1)}), bf16[16,16,8,376]{3,2,1,0:T(8,128)(2,1)S(1)}, u32[]{:S(2)}, u32[]{:S(2)}) async-start(bf16[16,16,8,376]{3,2,1,0:T(8,128)(2,1)} %reshape.61), calls=%async_computation | async-start | bytes 3145728 | tf_op jit(solution)/shard_map/all_to_all | solution.py:58
  24.5 439.1 %all-gather.2.cloned.1.call-start = ((), (), s32[]{:S(2)}) async-start(), calls=%async_computation.1 | async-start | bytes 7380992 | tf_op jit(solution)/shard_map/all_gather | solution.py:105
  24.8 1.3 collective-permute-start
  26.1 12.7 %collective-permute-start.1 = (f32[2,188,36]{1,2,0:T(8,128)S(1)}, f32[2,188,36]{1,2,0:T(8,128)S(1)}, u32[]{:S(2)}, u32[]{:S(2)}) collective-permute-start(f32[2,188,36]{1,2,0:T(8,128)S(1)} %add.104), channel_id=1, source_target_pairs={{0,2},{1,3},{2,0},{3,1},{4,6},{5,7},{6,4},{7,5},{8,10},{9,11},{10,... | collective-permute-start | bytes 162440 | tf_op jit(solution)/shard_map/ppermute | solution.py:56
  38.8 13.9 %collective-permute-start.2 = (f32[2,188,36]{1,2,0:T(8,128)S(1)}, f32[2,188,36]{1,2,0:T(8,128)S(1)}, u32[]{:S(2)}, u32[]{:S(2)}) collective-permute-start(f32[2,188,36]{1,2,0:T(8,128)S(1)} %add.105), channel_id=1, source_target_pairs={{0,4},{1,5},{2,6},{3,7},{4,0},{5,1},{6,2},{7,3},{8,12},{9,13},{10,... | collective-permute-start | bytes 162440 | tf_op jit(solution)/shard_map/ppermute | solution.py:56
  52.8 13.0 %collective-permute-start.3 = (f32[2,188,36]{1,2,0:T(8,128)S(1)}, f32[2,188,36]{1,2,0:T(8,128)S(1)}, u32[]{:S(2)}, u32[]{:S(2)}) collective-permute-start(f32[2,188,36]{1,2,0:T(8,128)S(1)} %add.106), channel_id=1, source_target_pairs={{0,8},{1,9},{2,10},{3,11},{4,12},{5,13},{6,14},{7,15},{8,0},{9,1},... | collective-permute-start | bytes 162440 | tf_op jit(solution)/shard_map/ppermute | solution.py:56
  74.4 5.4 %copy-start.1 = (f32[16,188,36]{1,2,0:T(8,128)S(1)}, f32[16,188,36]{1,2,0:T(8,128)}, u32[]{:S(2)}) copy-start(f32[16,188,36]{1,2,0:T(8,128)} %get-tuple-element.143) | copy-start | bytes 1299460 | tf_op jit(solution)/shard_map/while
  74.4 5.4 %copy-start.2 = (f32[16,188,36]{1,2,0:T(8,128)S(1)}, f32[16,188,36]{1,2,0:T(8,128)}, u32[]{:S(2)}) copy-start(f32[16,188,36]{1,2,0:T(8,128)} %get-tuple-element.144) | copy-start | bytes 1299460 | tf_op jit(solution)/shard_map/while
  90.5 5.4 %copy-start.1 = (f32[16,188,36]{1,2,0:T(8,128)S(1)}, f32[16,188,36]{1,2,0:T(8,128)}, u32[]{:S(2)}) copy-start(f32[16,188,36]{1,2,0:T(8,128)} %get-tuple-element.143) | copy-start | bytes 1299460 | tf_op jit(solution)/shard_map/while
  90.5 5.4 %copy-start.2 = (f32[16,188,36]{1,2,0:T(8,128)S(1)}, f32[16,188,36]{1,2,0:T(8,128)}, u32[]{:S(2)}) copy-start(f32[16,188,36]{1,2,0:T(8,128)} %get-tuple-element.144) | copy-start | bytes 1299460 | tf_op jit(solution)/shard_map/while
  106.6 5.4 %copy-start.1 = (f32[16,188,36]{1,2,0:T(8,128)S(1)}, f32[16,188,36]{1,2,0:T(8,128)}, u32[]{:S(2)}) copy-start(f32[16,188,36]{1,2,0:T(8,128)} %get-tuple-element.143) | copy-start | bytes 1299460 | tf_op jit(solution)/shard_map/while
  106.6 5.4 %copy-start.2 = (f32[16,188,36]{1,2,0:T(8,128)S(1)}, f32[16,188,36]{1,2,0:T(8,128)}, u32[]{:S(2)}) copy-start(f32[16,188,36]{1,2,0:T(8,128)} %get-tuple-element.144) | copy-start | bytes 1299460 | tf_op jit(solution)/shard_map/while
  122.7 5.4 %copy-start.1 = (f32[16,188,36]{1,2,0:T(8,128)S(1)}, f32[16,188,36]{1,2,0:T(8,128)}, u32[]{:S(2)}) copy-start(f32[16,188,36]{1,2,0:T(8,128)} %get-tuple-element.143) | copy-start | bytes 1299460 | tf_op jit(solution)/shard_map/while
  122.7 5.4 %copy-start.2 = (f32[16,188,36]{1,2,0:T(8,128)S(1)}, f32[16,188,36]{1,2,0:T(8,128)}, u32[]{:S(2)}) copy-start(f32[16,188,36]{1,2,0:T(8,128)} %get-tuple-element.144) | copy-start | bytes 1299460 | tf_op jit(solution)/shard_map/while
  138.8 5.4 %copy-start.1 = (f32[16,188,36]{1,2,0:T(8,128)S(1)}, f32[16,188,36]{1,2,0:T(8,128)}, u32[]{:S(2)}) copy-start(f32[16,188,36]{1,2,0:T(8,128)} %get-tuple-element.143) | copy-start | bytes 1299460 | tf_op jit(solution)/shard_map/while
  138.8 5.4 %copy-start.2 = (f32[16,188,36]{1,2,0:T(8,128)S(1)}, f32[16,188,36]{1,2,0:T(8,128)}, u32[]{:S(2)}) copy-start(f32[16,188,36]{1,2,0:T(8,128)} %get-tuple-element.144) | copy-start | bytes 1299460 | tf_op jit(solution)/shard_map/while
  154.9 5.4 %copy-start.1 = (f32[16,188,36]{1,2,0:T(8,128)S(1)}, f32[16,188,36]{1,2,0:T(8,128)}, u32[]{:S(2)}) copy-start(f32[16,188,36]{1,2,0:T(8,128)} %get-tuple-element.143) | copy-start | bytes 1299460 | tf_op jit(solution)/shard_map/while
  154.9 5.4 %copy-start.2 = (f32[16,188,36]{1,2,0:T(8,128)S(1)}, f32[16,188,36]{1,2,0:T(8,128)}, u32[]{:S(2)}) copy-start(f32[16,188,36]{1,2,0:T(8,128)} %get-tuple-element.144) | copy-start | bytes 1299460 | tf_op jit(solution)/shard_map/while
  171.0 5.4 %copy-start.1 = (f32[16,188,36]{1,2,0:T(8,128)S(1)}, f32[16,188,36]{1,2,0:T(8,128)}, u32[]{:S(2)}) copy-start(f32[16,188,36]{1,2,0:T(8,128)} %get-tuple-element.143) | copy-start | bytes 1299460 | tf_op jit(solution)/shard_map/while
  171.0 5.4 %copy-start.2 = (f32[16,188,36]{1,2,0:T(8,128)S(1)}, f32[16,188,36]{1,2,0:T(8,128)}, u32[]{:S(2)}) copy-start(f32[16,188,36]{1,2,0:T(8,128)} %get-tuple-element.144) | copy-start | bytes 1299460 | tf_op jit(solution)/shard_map/while
  187.1 5.4 %copy-start.1 = (f32[16,188,36]{1,2,0:T(8,128)S(1)}, f32[16,188,36]{1,2,0:T(8,128)}, u32[]{:S(2)}) copy-start(f32[16,188,36]{1,2,0:T(8,128)} %get-tuple-element.143) | copy-start | bytes 1299460 | tf_op jit(solution)/shard_map/while
  187.1 5.4 %copy-start.2 = (f32[16,188,36]{1,2,0:T(8,128)S(1)}, f32[16,188,36]{1,2,0:T(8,128)}, u32[]{:S(2)}) copy-start(f32[16,188,36]{1,2,0:T(8,128)} %get-tuple-element.144) | copy-start | bytes 1299460 | tf_op jit(solution)/shard_map/while
  203.2 5.4 %copy-start.1 = (f32[16,188,36]{1,2,0:T(8,128)S(1)}, f32[16,188,36]{1,2,0:T(8,128)}, u32[]{:S(2)}) copy-start(f32[16,188,36]{1,2,0:T(8,128)} %get-tuple-element.143) | copy-start | bytes 1299460 | tf_op jit(solution)/shard_map/while
  203.2 5.4 %copy-start.2 = (f32[16,188,36]{1,2,0:T(8,128)S(1)}, f32[16,188,36]{1,2,0:T(8,128)}, u32[]{:S(2)}) copy-start(f32[16,188,36]{1,2,0:T(8,128)} %get-tuple-element.144) | copy-start | bytes 1299460 | tf_op jit(solution)/shard_map/while
  219.2 5.4 %copy-start.1 = (f32[16,188,36]{1,2,0:T(8,128)S(1)}, f32[16,188,36]{1,2,0:T(8,128)}, u32[]{:S(2)}) copy-start(f32[16,188,36]{1,2,0:T(8,128)} %get-tuple-element.143) | copy-start | bytes 1299460 | tf_op jit(solution)/shard_map/while
  219.3 5.4 %copy-start.2 = (f32[16,188,36]{1,2,0:T(8,128)S(1)}, f32[16,188,36]{1,2,0:T(8,128)}, u32[]{:S(2)}) copy-start(f32[16,188,36]{1,2,0:T(8,128)} %get-tuple-element.144) | copy-start | bytes 1299460 | tf_op jit(solution)/shard_map/while
  235.3 5.4 %copy-start.1 = (f32[16,188,36]{1,2,0:T(8,128)S(1)}, f32[16,188,36]{1,2,0:T(8,128)}, u32[]{:S(2)}) copy-start(f32[16,188,36]{1,2,0:T(8,128)} %get-tuple-element.143) | copy-start | bytes 1299460 | tf_op jit(solution)/shard_map/while
  235.3 5.4 %copy-start.2 = (f32[16,188,36]{1,2,0:T(8,128)S(1)}, f32[16,188,36]{1,2,0:T(8,128)}, u32[]{:S(2)}) copy-start(f32[16,188,36]{1,2,0:T(8,128)} %get-tuple-element.144) | copy-start | bytes 1299460 | tf_op jit(solution)/shard_map/while
  251.4 5.4 %copy-start.1 = (f32[16,188,36]{1,2,0:T(8,128)S(1)}, f32[16,188,36]{1,2,0:T(8,128)}, u32[]{:S(2)}) copy-start(f32[16,188,36]{1,2,0:T(8,128)} %get-tuple-element.143) | copy-start | bytes 1299460 | tf_op jit(solution)/shard_map/while
  251.4 5.4 %copy-start.2 = (f32[16,188,36]{1,2,0:T(8,128)S(1)}, f32[16,188,36]{1,2,0:T(8,128)}, u32[]{:S(2)}) copy-start(f32[16,188,36]{1,2,0:T(8,128)} %get-tuple-element.144) | copy-start | bytes 1299460 | tf_op jit(solution)/shard_map/while
  267.5 5.4 %copy-start.1 = (f32[16,188,36]{1,2,0:T(8,128)S(1)}, f32[16,188,36]{1,2,0:T(8,128)}, u32[]{:S(2)}) copy-start(f32[16,188,36]{1,2,0:T(8,128)} %get-tuple-element.143) | copy-start | bytes 1299460 | tf_op jit(solution)/shard_map/while
  267.5 5.4 %copy-start.2 = (f32[16,188,36]{1,2,0:T(8,128)S(1)}, f32[16,188,36]{1,2,0:T(8,128)}, u32[]{:S(2)}) copy-start(f32[16,188,36]{1,2,0:T(8,128)} %get-tuple-element.144) | copy-start | bytes 1299460 | tf_op jit(solution)/shard_map/while
  283.6 5.4 %copy-start.1 = (f32[16,188,36]{1,2,0:T(8,128)S(1)}, f32[16,188,36]{1,2,0:T(8,128)}, u32[]{:S(2)}) copy-start(f32[16,188,36]{1,2,0:T(8,128)} %get-tuple-element.143) | copy-start | bytes 1299460 | tf_op jit(solution)/shard_map/while
  283.6 5.4 %copy-start.2 = (f32[16,188,36]{1,2,0:T(8,128)S(1)}, f32[16,188,36]{1,2,0:T(8,128)}, u32[]{:S(2)}) copy-start(f32[16,188,36]{1,2,0:T(8,128)} %get-tuple-element.144) | copy-start | bytes 1299460 | tf_op jit(solution)/shard_map/while
  299.7 5.4 %copy-start.1 = (f32[16,188,36]{1,2,0:T(8,128)S(1)}, f32[16,188,36]{1,2,0:T(8,128)}, u32[]{:S(2)}) copy-start(f32[16,188,36]{1,2,0:T(8,128)} %get-tuple-element.143) | copy-start | bytes 1299460 | tf_op jit(solution)/shard_map/while
  299.7 5.4 %copy-start.2 = (f32[16,188,36]{1,2,0:T(8,128)S(1)}, f32[16,188,36]{1,2,0:T(8,128)}, u32[]{:S(2)}) copy-start(f32[16,188,36]{1,2,0:T(8,128)} %get-tuple-element.144) | copy-start | bytes 1299460 | tf_op jit(solution)/shard_map/while
  315.8 5.4 %copy-start.1 = (f32[16,188,36]{1,2,0:T(8,128)S(1)}, f32[16,188,36]{1,2,0:T(8,128)}, u32[]{:S(2)}) copy-start(f32[16,188,36]{1,2,0:T(8,128)} %get-tuple-element.143) | copy-start | bytes 1299460 | tf_op jit(solution)/shard_map/while
  315.8 5.4 %copy-start.2 = (f32[16,188,36]{1,2,0:T(8,128)S(1)}, f32[16,188,36]{1,2,0:T(8,128)}, u32[]{:S(2)}) copy-start(f32[16,188,36]{1,2,0:T(8,128)} %get-tuple-element.144) | copy-start | bytes 1299460 | tf_op jit(solution)/shard_map/while
  331.9 5.4 %copy-start.1 = (f32[16,188,36]{1,2,0:T(8,128)S(1)}, f32[16,188,36]{1,2,0:T(8,128)}, u32[]{:S(2)}) copy-start(f32[16,188,36]{1,2,0:T(8,128)} %get-tuple-element.143) | copy-start | bytes 1299460 | tf_op jit(solution)/shard_map/while
  331.9 5.4 %copy-start.2 = (f32[16,188,36]{1,2,0:T(8,128)S(1)}, f32[16,188,36]{1,2,0:T(8,128)}, u32[]{:S(2)}) copy-start(f32[16,188,36]{1,2,0:T(8,128)} %get-tuple-element.144) | copy-start | bytes 1299460 | tf_op jit(solution)/shard_map/while
  348.0 5.4 %copy-start.2 = (f32[16,188,36]{1,2,0:T(8,128)S(1)}, f32[16,188,36]{1,2,0:T(8,128)}, u32[]{:S(2)}) copy-start(f32[16,188,36]{1,2,0:T(8,128)} %get-tuple-element.144) | copy-start | bytes 1299460 | tf_op jit(solution)/shard_map/while
  364.1 5.4 %copy-start.1 = (f32[16,188,36]{1,2,0:T(8,128)S(1)}, f32[16,188,36]{1,2,0:T(8,128)}, u32[]{:S(2)}) copy-start(f32[16,188,36]{1,2,0:T(8,128)} %get-tuple-element.143) | copy-start | bytes 1299460 | tf_op jit(solution)/shard_map/while
  364.1 5.4 %copy-start.2 = (f32[16,188,36]{1,2,0:T(8,128)S(1)}, f32[16,188,36]{1,2,0:T(8,128)}, u32[]{:S(2)}) copy-start(f32[16,188,36]{1,2,0:T(8,128)} %get-tuple-element.144) | copy-start | bytes 1299460 | tf_op jit(solution)/shard_map/while
  380.2 5.4 %copy-start.1 = (f32[16,188,36]{1,2,0:T(8,128)S(1)}, f32[16,188,36]{1,2,0:T(8,128)}, u32[]{:S(2)}) copy-start(f32[16,188,36]{1,2,0:T(8,128)} %get-tuple-element.143) | copy-start | bytes 1299460 | tf_op jit(solution)/shard_map/while
  380.2 5.4 %copy-start.2 = (f32[16,188,36]{1,2,0:T(8,128)S(1)}, f32[16,188,36]{1,2,0:T(8,128)}, u32[]{:S(2)}) copy-start(f32[16,188,36]{1,2,0:T(8,128)} %get-tuple-element.144) | copy-start | bytes 1299460 | tf_op jit(solution)/shard_map/while
  (22 other events, 72.4 us)
Sparse Core Ops, SparseCore 0:
  399.3 64.2 all-gather.1
